TPU v7x, 32 devices: a whole 2x2x4 slice. The times are simulated.
32 devices in a mesh: seq: 4 (over y, x), tp: 8 (over z, core).
Axes of the slice: x: 2, y: 2, z: 4, core: 2. Of those that a mesh axis runs over, the one named last changes fastest.
Arguments:
- hidden: bfloat16 [4096, 4096], P(('seq', 'tp')), may hold values from -6 to 6
- norm_gain: float32 [4096], replicated, may hold values from 0.5 to 1.5
- inner_weight: bfloat16 [4096, 2, 2048], P(None, None, 'tp'), may hold values from -0.09375 to 0.09375
- group_weight: bfloat16 [4096, 1024], P(None, 'tp'), may hold values from -0.09375 to 0.09375
- step_weight: bfloat16 [4096, 32], P(None, 'tp'), may hold values from -0.09375 to 0.09375
- step_bias: float32 [32], P('tp'), may hold values from -2 to 1
- decay_rate: float32 [32], P('tp'), may hold values from 0.0001 to 0.1
- filter_inner: bfloat16 [4, 2048], P(None, 'tp'), may hold values from -3 to 3
- filter_group: bfloat16 [4, 1024], P(None, 'tp'), may hold values from -3 to 3
- skip_gain: float32 [32], P('tp'), may hold values from 0.5 to 1.5
- mixer_gain: float32 [2048], P('tp'), may hold values from 0.5 to 1.5
- output_weight: bfloat16 [2048, 4096], P('tp'), may hold values from -0.125 to 0.125
- segment_ids: int32 [4096], replicated, may hold values from 0 to 3, never falling along the last dimension, each value on 1 to 2048 neighbouring positions
Outputs:
- layer_out: bfloat16 [4096, 4096], P(('seq', 'tp'))
Inputs may be any that keep to these rules, and one draw needn't show every extreme that they name: `segment_ids`: ids never fall along the pack; every id names at least one token, and one request has exactly 2048 tokens.
All inputs are finite; a program needn't handle non-finite values.
Results may differ from a plain program's by a relative error of at most 0.0051.
Values may be sent and summed in bfloat16 or wider, within the bound.
A program may use at most 128 MiB of HBM per device.

v0:
```python
import jax
import jax.numpy as jnp
from jax import lax
from jax.sharding import PartitionSpec as P

STRETCH = 256
EPS = 1e-05
HIGH = lax.Precision.HIGHEST


def swapped(block, axis, stride):
    count = lax.axis_size(axis)
    route = []
    for low in range(count):
        high = low | 1 << stride
        if high != low and high < count:
            route += [(low, high), (high, low)]
    return lax.ppermute(block, axis, route)


def from_behind(array, axis, by):
    size = lax.axis_size(axis)
    pairs = [(i, i + by) for i in range(size) if 0 <= i + by < size]
    return lax.ppermute(array, axis, pairs)


def entering_2(value, axis, join, neutral):
    count, mine = (lax.axis_size(axis), lax.axis_index(axis))
    pieces = jax.tree.map(lambda part: lax.all_gather(part, axis), value)
    total = jax.tree.map(
        lambda part, zero: jnp.full_like(part, 0) + jnp.asarray(zero, part.dtype), value, neutral
    )

    def hop(position, total):
        longer = join(total, jax.tree.map(lambda part: part[position], pieces))
        return jax.tree.map(lambda new, old: jnp.where(position < mine, new, old), longer, total)

    return lax.fori_loop(0, count - 1, hop, total)


def combine(earlier, later):
    return (earlier[0] * later[0], later[0][:, None, None] * earlier[1] + later[1])


def body(
    hidden,
    norm_gain,
    inner_weight,
    group_weight,
    step_weight,
    step_bias,
    decay_rate,
    filter_inner,
    filter_group,
    skip_gain,
    mixer_gain,
    output_weight,
    segment_ids,
):
    rows = hidden.shape[0]
    length = rows * lax.axis_size("tp")
    width = hidden.shape[1]
    inner_dev = inner_weight.shape[2]
    heads_dev = step_weight.shape[1]
    head_dim = inner_dev // heads_dev
    state_dim = group_weight.shape[1]
    taps = filter_inner.shape[0]
    first_row = lax.axis_index("seq") * length
    is_first = lax.axis_index("tp") % 2 == 0
    hidden_f = hidden.astype(jnp.float32)
    normed = (
        hidden_f
        * lax.rsqrt(jnp.mean(hidden_f * hidden_f, axis=-1, keepdims=True) + EPS)
        * norm_gain
    ).astype(jnp.bfloat16)
    other_weight, other_filter = swapped((group_weight, filter_group), "tp", 0)
    group_cols = (
        jnp.where(is_first, group_weight, other_weight),
        jnp.where(is_first, other_weight, group_weight),
    )
    filters = jnp.concatenate(
        [
            filter_inner,
            jnp.where(is_first, filter_group, other_filter),
            jnp.where(is_first, other_filter, filter_group),
        ],
        axis=1,
    )
    matrices = (inner_weight.reshape(width, 2 * inner_dev),) + group_cols + (step_weight,)
    piece = lax.all_gather(normed, "tp", axis=0, tiled=True)
    projected = jnp.concatenate(
        [jnp.dot(piece, matrix, preferred_element_type=jnp.float32) for matrix in matrices], axis=1
    )
    gate_z = projected[:, :inner_dev]
    conv_in = projected[:, inner_dev:-heads_dev]
    step_raw = projected[:, -heads_dev:]
    seg_pad = jnp.concatenate([jnp.full((taps - 1,), -1, jnp.int32), segment_ids])
    seg_ext = lax.dynamic_slice_in_dim(seg_pad, first_row, length + taps - 1)
    seg_local = seg_ext[taps - 1 :]
    before = from_behind(conv_in[length - (taps - 1) :], "seq", 1)
    extended = jnp.concatenate([before, conv_in], axis=0)
    filters_f = filters.astype(jnp.float32)
    total = jnp.zeros_like(conv_in)
    for offset in range(taps):
        same = (seg_ext[offset : offset + length] == seg_local).astype(jnp.float32)
        total = total + filters_f[offset] * extended[offset : offset + length] * same[:, None]
    active = jax.nn.silu(total)
    inner_x = active[:, :inner_dev]
    input_map = active[:, inner_dev : inner_dev + state_dim]
    output_map = active[:, inner_dev + state_dim :]
    starts = seg_local != seg_ext[taps - 2 : taps - 2 + length]
    step = jax.nn.softplus(step_raw + step_bias)
    log_decay = -step * decay_rate
    blocks = length // STRETCH
    block_x = inner_x.reshape(blocks, STRETCH, heads_dev, head_dim)
    block_b = input_map.reshape(blocks, STRETCH, state_dim)
    block_c = output_map.reshape(blocks, STRETCH, state_dim)
    step_heads = step.reshape(blocks, STRETCH, heads_dev).transpose(0, 2, 1)
    cumul = jnp.cumsum(log_decay.reshape(blocks, STRETCH, heads_dev), axis=1).transpose(0, 2, 1)
    block_seg = seg_local.reshape(blocks, STRETCH)
    block_start = starts.reshape(blocks, STRETCH)
    causal = jnp.tril(jnp.ones((STRETCH, STRETCH), jnp.bool_))
    same_seg = ((block_seg[:, :, None] == block_seg[:, None, :]) & causal)[:, None]
    gaps = cumul[:, :, :, None] - cumul[:, :, None, :]
    decay = jnp.where(same_seg, jnp.exp(jnp.where(same_seg, gaps, 0.0)), 0.0)
    products = jnp.einsum("cin,cjn->cij", block_c, block_b, precision=HIGH)
    mixing = decay * products[:, None] * step_heads[:, :, None, :]
    local_y = jnp.einsum("chij,cjhp->cihp", mixing, block_x, precision=HIGH)
    same_last = (block_seg == block_seg[:, -1:])[:, None, :]
    last_gap = cumul[:, :, -1:] - cumul
    end_weight = (
        jnp.where(same_last, jnp.exp(jnp.where(same_last, last_gap, 0.0)), 0.0) * step_heads
    )
    block_state = jnp.einsum("chj,cjhp,cjn->chpn", end_weight, block_x, block_b, precision=HIGH)
    clean = jnp.logical_not(jnp.any(block_start, axis=1)).astype(jnp.float32)
    block_keep = jnp.exp(cumul[:, :, -1]) * clean[:, None]

    def carry_blocks(carry, inputs):
        acc_state, acc_keep = carry
        keep, fresh = inputs
        return ((keep[:, None, None] * acc_state + fresh, acc_keep * keep), (acc_state, acc_keep))

    empty_state = jnp.zeros((heads_dev, head_dim, state_dim), jnp.float32)
    unit_keep = jnp.ones((heads_dev,), jnp.float32)
    (device_state, device_keep), (prior_state, prior_keep) = lax.scan(
        carry_blocks, (empty_state, unit_keep), (block_keep, block_state)
    )
    entering = entering_2((device_keep, device_state), "seq", combine, (unit_keep, empty_state))
    incoming = entering[1]
    entry_state = prior_state + prior_keep[:, :, None, None] * incoming[None]
    alive = (jnp.cumsum(block_start.astype(jnp.int32), axis=1) == 0).astype(jnp.float32)
    entry_weight = jnp.exp(cumul) * alive[:, None, :]
    carried_y = jnp.einsum("chi,cin,chpn->cihp", entry_weight, block_c, entry_state, precision=HIGH)
    ssm_out = (local_y + carried_y).reshape(length, heads_dev, head_dim) + skip_gain[
        None, :, None
    ] * inner_x.reshape(length, heads_dev, head_dim)
    gated = ssm_out.reshape(length, inner_dev) * jax.nn.silu(gate_z)
    own_squares = jnp.sum(gated * gated, axis=-1)
    other_squares = swapped(own_squares, "tp", 0)
    group_mean = (own_squares + other_squares) / (2 * inner_dev)
    mixed = (gated * lax.rsqrt(group_mean + EPS)[:, None] * mixer_gain).astype(jnp.bfloat16)
    partial_out = jnp.dot(mixed, output_weight, preferred_element_type=jnp.float32)
    mine = lax.psum_scatter(partial_out, "tp", scatter_dimension=0, tiled=True)
    return (hidden_f + mine).astype(jnp.bfloat16)


def solution(mesh):
    in_specs = (
        P(("seq", "tp"), None),
        P(),
        P(None, None, "tp"),
        P(None, "tp"),
        P(None, "tp"),
        P("tp"),
        P("tp"),
        P(None, "tp"),
        P(None, "tp"),
        P("tp"),
        P("tp"),
        P("tp", None),
        P(),
    )
    out_specs = P(("seq", "tp"), None)
    return jax.shard_map(body, mesh=mesh, in_specs=in_specs, out_specs=out_specs, check_vma=False)
```

profile of v0, /device:TPU:0, one launch (start us, length us, event | category | flops | bytes accessed | tf_op | source)
XLA Modules:
  0.0 372.5 jit_solution(9451892559120451516)
XLA Ops:
  6.6 1.7 fusion.20
  8.3 2.5 fusion.22
  11.6 1.2 reduce-window.16
  14.8 4.9 %copy.92 = bf16[512,8,2,256]{3,1,2,0:T(8,128)(2,1)} copy(bf16[512,8,2,256]{3,2,1,0:T(2,128)(2,1)} %bitcast.91) | data formatting | bytes 8388608
  21.1 74.7 %all-gather.4.cloned.1.call-done = bf16[1024,4096]{1,0:T(8,128)(2,1)} async-done(((bf16[128,4096]{1,0:T(8,128)(2,1)}), bf16[1024,4096]{1,0:T(8,128)(2,1)}) %all-gather.4.cloned.1.call-update) | async-done | bytes 8388624 | tf_op jit(solution)/shard_map/all_gather | solution.py:90
  95.8 5.7 %negate_multiply_fusion = (f32[1024,4]{0,1:T(4,128)S(1)}, f32[1024,4]{0,1:T(4,128)S(1)}) fusion(f32[4]{0:T(128)S(1)} %copy-done.15, f32[4]{0:T(128)S(1)} %copy-done.16, bf16[1024,4096]{1,0:T(8,128)(2,1)} %all-gather.4.cloned.1.call-done, bf16[4096,4]{0,1:T(4,128)(2,1)S(1)} %copy-done.13), kind=kOutput, calls=%fused_computation.96 | convolution fusion | flops 33591296 | bytes 8454176 | tf_op jit(solution)/shard_map/dot_general | solution.py:92
  101.5 4.8 %reduce-window.14 = f32[4,4,2,128]{3,2,1,0:T(2,128)S(1)} reduce-window(f32[4,4,2,128]{3,2,1,0:T(2,128)S(1)} %copy.83, f32[]{:T(128)} %constant.89.clone.1), window={size=1x1x1x128 pad=0_0x0_0x0_0x127_0}, to_apply=%region_1.2 | reduce-window | flops 520192 | bytes 32772 | tf_op jit(solution)/shard_map/reduce-window
  107.2 6.7 %fusion.38 = f32[1024,128]{0,1:T(8,128)S(1)} fusion(bf16[1024,4096]{1,0:T(8,128)(2,1)} %all-gather.4.cloned.1.call-done, bf16[4096,128]{1,0:T(8,128)(2,1)} %collective-permute-done.1, bf16[4096,128]{1,0:T(8,128)(2,1)S(1)} %copy-done.7, pred[]{:T(512)S(6)} %eq.59), kind=kOutput, calls=%fused_computation.58 | convolution fusion | flops 1074266112 | bytes 11010049 | tf_op jit(solution)/shard_map/dot_general | solution.py:92
  113.8 2.9 fusion.40
  116.8 6.5 %fusion.78 = f32[1024,512]{0,1:T(8,128)S(1)} fusion(bf16[1024,4096]{1,0:T(8,128)(2,1)S(1)} %copy-done.1, bf16[4096,512]{1,0:T(8,128)(2,1)} %bitcast.92), kind=kOutput, calls=%fused_computation.123 | convolution fusion | flops 4294967296 | bytes 14680064 | tf_op jit(solution)/shard_map/dot_general | solution.py:92
  123.4 3.6 collective-permute-start.2
  127.4 5.9 %collective-permute-done.2 = f32[3,512]{0,1:T(8,128)S(1)} collective-permute-done((f32[3,512]{0,1:T(8,128)S(1)}, f32[3,512]{0,1:T(8,128)S(1)}, u32[]{:S(2)}, u32[]{:S(2)}) %collective-permute-start.2) | collective-permute-done | bytes 6176 | tf_op jit(solution)/shard_map/ppermute | solution.py:24
  133.3 2.4 divide_multiply_fusion
  137.4 2.7 reshape.145
  141.1 3.4 fusion.36
  144.5 6.9 %while.31 = (s32[]{:T(128)}, f32[4,64,128]{2,1,0:T(8,128)S(1)}, f32[4]{0:T(128)S(1)}, f32[4,4,64,128]{3,2,1,0:T(8,128)}, f32[4,4]{1,0:T(4,128)S(1)}, /*index=5*/...) while((s32[]{:T(128)}, f32[4,64,128]{2,1,0:T(8,128)S(1)}, f32[4]{0:T(128)S(1)}, ...), condition=%wide.region_7.8_spmd.clone, body=%wide.region_6.7_spmd.clone.sunk | while | flops 131083 | bytes 655617 | solution.py:145
  152.7 10.8 %all-reduce.1 = f32[16]{0:T(128)S(1)} all-reduce(f32[16]{0:T(128)S(1)} %dynamic-update-slice), channel_id=2, replica_groups=mesh['seq'=4,'tp'=8] {'seq'}, use_global_device_ids=true, to_apply=%add.1 | all-reduce | flops 16 | bytes 128
  163.6 10.2 %all-gather.1 = f32[16,64,128]{2,1,0:T(8,128)} all-gather(f32[4,64,128]{2,1,0:T(8,128)S(1)} %get-tuple-element.142), channel_id=3, replica_groups=mesh['seq'=4,'tp'=8] {'seq'}, dimensions={0}, use_global_device_ids=true | all-gather | bytes 655360 | tf_op jit(solution)/shard_map/all_gather | solution.py:29
  173.8 3.1 while.32
  178.2 5.2 %fusion.33 = f32[4,256,4,64]{1,3,2,0:T(8,128)S(1)} fusion(f32[4,4,256]{2,1,0:T(4,128)S(1)} %copy.69, f32[4,256,256]{2,1,0:T(8,128)S(1)} %fusion.47, f32[4,4,256]{2,1,0:T(4,128)S(1)} %reduce_window_sum.41, pred[4,256,256]{2,1,0:T(8,128)(4,1)S(1)} %copy-done.11, f32[4,256,4,64]{1,0,3,2:T(4,128)S(1)} %copy-done.8), kind=kOutput, calls=%fused_computation.51 | convolution fusion | flops 810549248 | bytes 3440640 | tf_op jit(solution)/shard_map/chij,cjhp->cihp/dot_general | solution.py:128
  187.3 1.2 collective-permute-done.3
  188.4 8.2 %fusion.46 = f32[1024,4096]{1,0:T(8,128)} fusion(bf16[256,4096]{1,0:T(8,128)(2,1)S(1)} %copy-done, f32[1024,256]{0,1:T(8,128)S(1)} %get-tuple-element.213, f32[256]{0:T(256)S(1)} %copy-done.14, f32[1024]{0:T(1024)S(1)} %add_rsqrt_fusion), kind=kOutput, calls=%fused_computation.67 | convolution fusion | flops 2148270080 | bytes 19928064 | tf_op jit(solution)/shard_map/dot_general | solution.py:162
  196.7 166.2 %reduce-scatter.2.cloned.1.call-done = f32[128,4096]{1,0:T(8,128)} async-done(((f32[1024,4096]{1,0:T(8,128)}), f32[128,4096]{1,0:T(8,128)}) %reduce-scatter.2.cloned.1.call-update) | async-done | bytes 2097168 | tf_op jit(solution)/shard_map/reduce_scatter | solution.py:163
  362.8 2.8 fusion.23
  (135 shorter events, 23.7 us)
Async XLA Ops:
  6.5 181.9 %copy-start = (bf16[256,4096]{1,0:T(8,128)(2,1)S(1)}, bf16[256,4096]{1,0:T(8,128)(2,1)}, u32[]{:S(2)}) copy-start(bf16[256,4096]{1,0:T(8,128)(2,1)} %param.28) | copy-start | bytes 6291460
  6.5 4.3 %copy-start.18 = (bf16[4,128]{1,0:T(4,128)(2,1)S(1)}, bf16[4,128]{1,0:T(4,128)(2,1)}, u32[]{:S(2)}) copy-start(bf16[4,128]{1,0:T(4,128)(2,1)} %param.25) | copy-start | bytes 3076
  6.5 4.9 %copy-start.7 = (bf16[4096,128]{1,0:T(8,128)(2,1)S(1)}, bf16[4096,128]{1,0:T(8,128)(2,1)}, u32[]{:S(2)}) copy-start(bf16[4096,128]{1,0:T(8,128)(2,1)} %param.20) | copy-start | bytes 3145732
  6.5 5.0 %copy-start.12 = (s32[4096]{0:T(1024)S(1)}, s32[4096]{0:T(1024)}, u32[]{:S(2)}) copy-start(s32[4096]{0:T(1024)} %param.29) | copy-start | bytes 49156
  6.5 89.2 %all-gather.4.cloned.1.call-start = ((), (), s32[]{:S(2)}) async-start(), calls=%async_computation.1 | async-start | bytes 9437184 | tf_op jit(solution)/shard_map/all_gather | solution.py:90
  8.3 6.3 %copy-start.19 = (f32[4]{0:T(128)S(1)}, f32[4]{0:T(128)}, u32[]{:S(2)}) copy-start(f32[4]{0:T(128)} %param.26) | copy-start | bytes 52
  10.8 352.0 %reduce-scatter.2.cloned.1.call-start = ((), (), s32[]{:S(2)}) async-start(), calls=%async_computation.2 | async-start | bytes 18874368 | tf_op jit(solution)/shard_map/reduce_scatter | solution.py:163
  10.9 10.1 %collective-permute-start = (bf16[4,128]{1,0:T(4,128)(2,1)S(1)}, bf16[4,128]{1,0:T(4,128)(2,1)S(1)}, u32[]{:S(2)}, u32[]{:S(2)}) collective-permute-start(bf16[4,128]{1,0:T(4,128)(2,1)S(1)} %copy-done.18), channel_id=1, source_target_pairs={{0,1},{1,0},{2,3},{3,2},{4,5},{5,4},{6,7},{7,6},{8,9},{9,8},{10,11... | collective-permute-start | bytes 3080 | tf_op jit(solution)/shard_map/ppermute | solution.py:18
  11.4 95.7 %collective-permute-start.1 = (bf16[4096,128]{1,0:T(8,128)(2,1)S(1)}, bf16[4096,128]{1,0:T(8,128)(2,1)}, u32[]{:S(2)}, u32[]{:S(2)}) collective-permute-start(bf16[4096,128]{1,0:T(8,128)(2,1)S(1)} %copy-done.7), channel_id=1, source_target_pairs={{0,1},{1,0},{2,3},{3,2},{4,5},{5,4},{6,7},{7,6},{8,9},{9,8},{10,11... | collective-permute-start | bytes 3145736 | tf_op jit(solution)/shard_map/ppermute | solution.py:18
  14.8 5.0 %copy-start.20 = (u32[32]{0:T(128)S(1)}, u32[32]{0:T(128)}, u32[]{:S(2)}) copy-start(u32[32]{0:T(128)} %constant.107) | copy-start | bytes 388
  14.8 6.3 %copy-start.17 = (bf16[4,256]{1,0:T(4,128)(2,1)S(1)}, bf16[4,256]{1,0:T(4,128)(2,1)}, u32[]{:S(2)}) copy-start(bf16[4,256]{1,0:T(4,128)(2,1)} %param.24) | copy-start | bytes 6148
  14.8 81.0 %copy-start.13 = (bf16[4096,4]{0,1:T(4,128)(2,1)S(1)}, bf16[4096,4]{0,1:T(4,128)(2,1)}, u32[]{:S(2)}) copy-start(bf16[4096,4]{0,1:T(4,128)(2,1)} %param.21) | copy-start | bytes 98308
  14.8 81.0 %copy-start.15 = (f32[4]{0:T(128)S(1)}, f32[4]{0:T(128)}, u32[]{:S(2)}) copy-start(f32[4]{0:T(128)} %param.23) | copy-start | bytes 52
  14.8 81.0 %copy-start.16 = (f32[4]{0:T(128)S(1)}, f32[4]{0:T(128)}, u32[]{:S(2)}) copy-start(f32[4]{0:T(128)} %param.22) | copy-start | bytes 52
  107.1 6.7 %copy-start.1 = (bf16[1024,4096]{1,0:T(8,128)(2,1)S(1)}, bf16[1024,4096]{1,0:T(8,128)(2,1)}, u32[]{:S(2)}) copy-start(bf16[1024,4096]{1,0:T(8,128)(2,1)} %all-gather.4.cloned.1.call-done) | copy-start | bytes 25165828
  123.3 4.1 %copy-start.4 = (f32[1024,512]{0,1:T(8,128)}, f32[1024,512]{0,1:T(8,128)S(1)}, u32[]{:S(2)}) copy-start(f32[1024,512]{0,1:T(8,128)S(1)} %fusion.78) | copy-start | bytes 6291460
  123.4 9.8 %collective-permute-start.2 = (f32[3,512]{0,1:T(8,128)S(1)}, f32[3,512]{0,1:T(8,128)S(1)}, u32[]{:S(2)}, u32[]{:S(2)}) collective-permute-start(f32[3,512]{0,1:T(8,128)S(1)} %pad_maximum_fusion.3), channel_id=1, source_target_pairs={{0,8},{8,16},{16,24},{1,9},{9,17},{17,25},{2,10},{10,18},{18,26},{... | collective-permute-start | bytes 18440 | tf_op jit(solution)/shard_map/ppermute | solution.py:24
  135.6 1.6 copy-start.2
  178.2 5.2 %copy-start.9 = (f32[4,256,128]{1,0,2:T(4,128)S(1)}, f32[4,256,128]{1,0,2:T(4,128)}, u32[]{:S(2)}) copy-start(f32[4,256,128]{1,0,2:T(4,128)} %reshape.149) | copy-start | bytes 1572868
  178.2 5.2 %copy-start.10 = (f32[4,4,64,128]{3,2,1,0:T(8,128)S(1)}, f32[4,4,64,128]{3,2,1,0:T(8,128)}, u32[]{:S(2)}) copy-start(f32[4,4,64,128]{3,2,1,0:T(8,128)} %get-tuple-element.139) | copy-start | bytes 1572868
  184.6 2.2 copy-start.5
  186.8 1.7 copy-start.14
  187.2 1.2 collective-permute-start.3
  196.7 166.2 %copy-start.6 = (bf16[128,4096]{1,0:T(8,128)(2,1)S(1)}, bf16[128,4096]{1,0:T(8,128)(2,1)}, u32[]{:S(2)}) copy-start(bf16[128,4096]{1,0:T(8,128)(2,1)} %param.17) | copy-start | bytes 3145732
  (3 other events, 4.1 us)
Sparse Core Ops, SparseCore 0:
  10.9 84.7 all-gather.3
  196.8 165.9 reduce-scatter.1
where the time goes:
time: 373 us; the launch traced here: 372 us
  waiting for transfers between devices  248 us (66%)
  matrix products  40.7 us (11%)
  other arithmetic  27.4 us (7%)
  blocking collectives  21.1 us (6%)
  local copies, waits for them, and re-layouts  16.4 us (4%)
  between operations  14.5 us (4%)
  starting transfers between devices  4.37 us (1%)
    reduce_scatter x1, waiting for transfers between devices, body(): mine = lax.psum_scatter(partial_out, 'tp', scatter_dimension=0, tiled=True)  166 us
    all_gather x1, waiting for transfers between devices, body(): piece = lax.all_gather(normed, 'tp', axis=0, tiled=True)  74.7 us
    dot_general x4, matrix products, body(): jnp.dot(piece, matrix, preferred_element_type=jnp.float32)  21.8 us
    unnamed x1, blocking collectives  10.8 us
    all_gather x1, blocking collectives, entering_2(): pieces = jax.tree.map(lambda part: lax.all_gather(part, axis), value)  10.2 us
    unnamed x49, local copies, waits for them, and re-layouts  8.25 us
    dot_general x1, matrix products, body(): jnp.dot(mixed, output_weight, preferred_element_type=jnp.float32)  8.21 us
  transfers between devices with their start and end apart: 6, of which 4 were waited for; matrix products, arithmetic and copies ran while one was open for 5% of the time, Pallas kernels for 0%

commit v1 on v0

--- a/solution.py
+++ b/solution.py
@@ -87,7 +87,14 @@
         axis=1,
     )
     matrices = (inner_weight.reshape(width, 2 * inner_dev),) + group_cols + (step_weight,)
-    piece = lax.all_gather(normed, "tp", axis=0, tiled=True)
+    ways, here, hop_2 = (lax.axis_size("tp"), lax.axis_index("tp"), normed.shape[0])
+    line, have = (normed, 1)
+    while have < ways:
+        line = jnp.concatenate(
+            [line, lax.ppermute(line, "tp", [(d, (d - have) % ways) for d in range(ways)])], axis=0
+        )
+        have = 2 * have
+    piece = jnp.roll(line, here * hop_2, axis=0)
     projected = jnp.concatenate(
         [jnp.dot(piece, matrix, preferred_element_type=jnp.float32) for matrix in matrices], axis=1
     )

time: 373 us -> 557 us (1.49)
  waiting for transfers between devices: 248 us -> 398 us
  local copies, waits for them, and re-layouts: 16.4 us -> 34.8 us
  matrix products: 40.7 us -> 48 us
  starting transfers between devices: 4.37 us -> 10 us
    ppermute x0 -> x3, waiting for transfers between devices: none -> 226 us  [body(): lax.ppermute(line, 'tp', [(d, (d - have) % ways) for d in range(ways)])]
    all_gather x1 -> x0, waiting for transfers between devices: 74.7 us -> none  [body(): piece = lax.all_gather(normed, 'tp', axis=0, tiled=True)]
    unnamed x49 -> x55, local copies, waits for them, and re-layouts: 8.25 us -> 22 us
    dot_general x4, matrix products: 21.8 us -> 27.7 us  [body(): jnp.dot(piece, matrix, preferred_element_type=jnp.float32)]
  transfers between devices with their start and end apart: 6 -> 8, of which waited for: 4 -> 6; matrix products, arithmetic and copies ran while one was open for 5% -> 8% of each run, Pallas kernels for 0% -> 0%
where the time goes in v1:
time: 557 us
  waiting for transfers between devices  398 us (71%)
  matrix products  48 us (9%)
  local copies, waits for them, and re-layouts  34.8 us (6%)
  other arithmetic  29.8 us (5%)
  blocking collectives  21.5 us (4%)
  between operations  14.5 us (3%)
  starting transfers between devices  10 us (2%)
    ppermute x3, waiting for transfers between devices, body(): lax.ppermute(line, 'tp', [(d, (d - have) % ways) for d in range(ways)])  226 us
    reduce_scatter x1, waiting for transfers between devices, body(): mine = lax.psum_scatter(partial_out, 'tp', scatter_dimension=0, tiled=True)  166 us
    dot_general x4, matrix products, body(): jnp.dot(piece, matrix, preferred_element_type=jnp.float32)  27.7 us
    unnamed x55, local copies, waits for them, and re-layouts  22 us
    all_gather x1, blocking collectives, entering_2(): pieces = jax.tree.map(lambda part: lax.all_gather(part, axis), value)  12.6 us
  transfers between devices with their start and end apart: 8, of which 6 were waited for; matrix products, arithmetic and copies ran while one was open for 8% of the time, Pallas kernels for 0%

profile of v1, /device:TPU:0, one launch (start us, length us, event | category | flops | bytes accessed | tf_op | source)
XLA Modules:
  0.0 556.6 jit_solution(12788775503215664028)
XLA Ops:
  10.8 4.5 collective-permute-start.1
  15.3 12.3 %collective-permute-done.1 = bf16[128,4096]{1,0:T(8,128)(2,1)S(1)} collective-permute-done((bf16[128,4096]{1,0:T(8,128)(2,1)S(1)}, bf16[128,4096]{1,0:T(8,128)(2,1)S(1)}, u32[]{:S(2)}, u32[]{:S(2)}) %collective-permute-start.1) | collective-permute-done | bytes 1048608 | tf_op jit(solution)/shard_map/ppermute | solution.py:94
  28.5 45.8 %collective-permute-done.2 = bf16[256,4096]{1,0:T(8,128)(2,1)S(1)} collective-permute-done((bf16[256,4096]{1,0:T(8,128)(2,1)S(1)}, bf16[256,4096]{1,0:T(8,128)(2,1)S(1)}, u32[]{:S(2)}, u32[]{:S(2)}) %collective-permute-start.2) | collective-permute-done | bytes 2097184 | tf_op jit(solution)/shard_map/ppermute | solution.py:94
  82.2 4.9 copy.92
  90.9 3.1 constant_dynamic-update-slice_fusion.5
  94.0 167.6 %collective-permute-done.3 = bf16[512,4096]{1,0:T(8,128)(2,1)} collective-permute-done((bf16[512,4096]{1,0:T(8,128)(2,1)}, bf16[512,4096]{1,0:T(8,128)(2,1)}, u32[]{:S(2)}, u32[]{:S(2)}) %collective-permute-start.3) | collective-permute-done | bytes 4194336 | tf_op jit(solution)/shard_map/ppermute | solution.py:94
  261.6 4.7 constant_dynamic-update-slice_fusion.4
  269.9 4.7 constant_dynamic-update-slice_fusion
  274.6 5.7 %negate_multiply_fusion = (f32[1024,4]{0,1:T(4,128)S(1)}, f32[1024,4]{0,1:T(4,128)S(1)}) fusion(f32[4]{0:T(128)S(1)} %copy-done.15, f32[4]{0:T(128)S(1)} %copy-done.16, bf16[4096,4]{0,1:T(4,128)(2,1)S(1)} %copy-done.13, bf16[2048,4096]{1,0:T(8,128)(2,1)} %constant_dynamic-update-slice_fusion, s32[]{:T(128)S(6)} %select_n.93), kind=kOutput, calls=%fused_computation.112 | convolution fusion | flops 33591296 | bytes 8454180 | tf_op jit(solution)/shard_map/dot_general | solution.py:99
  280.3 4.8 reduce-window.14
  285.9 8.3 %fusion.10 = f32[1024,512]{0,1:T(8,128)S(1)} fusion(bf16[4096,512]{1,0:T(8,128)(2,1)} %bitcast.88, bf16[2048,4096]{1,0:T(8,128)(2,1)} %constant_dynamic-update-slice_fusion, s32[]{:T(128)S(6)} %select_n.93), kind=kOutput, calls=%fused_computation.16 | convolution fusion | flops 4294967296 | bytes 14680068 | tf_op jit(solution)/shard_map/dot_general | solution.py:99
  294.2 7.3 %fusion.6 = f32[1024,128]{0,1:T(8,128)S(1)} fusion(bf16[2048,4096]{1,0:T(8,128)(2,1)} %constant_dynamic-update-slice_fusion, s32[]{:T(128)S(6)} %select_n.93, bf16[4096,128]{1,0:T(8,128)(2,1)} %collective-permute-done.4, bf16[4096,128]{1,0:T(8,128)(2,1)} %param.20, pred[]{:T(512)S(6)} %eq.62), kind=kOutput, calls=%fused_computation.12 | convolution fusion | flops 1074266112 | bytes 11010053 | tf_op jit(solution)/shard_map/dot_general | solution.py:99
  301.5 6.5 %fusion.8 = f32[1024,128]{0,1:T(8,128)S(1)} fusion(bf16[2048,4096]{1,0:T(8,128)(2,1)} %constant_dynamic-update-slice_fusion, s32[]{:T(128)S(6)} %select_n.93, bf16[4096,128]{1,0:T(8,128)(2,1)} %param.20, bf16[4096,128]{1,0:T(8,128)(2,1)} %collective-permute-done.4, pred[]{:T(512)S(6)} %eq.62), kind=kOutput, calls=%fused_computation.14 | convolution fusion | flops 1074266112 | bytes 11010053 | tf_op jit(solution)/shard_map/dot_general | solution.py:99
  308.2 3.6 collective-permute-start.5
  312.1 5.2 collective-permute-done.5
  325.2 3.4 fusion.47
  328.5 6.8 %while.31 = (s32[]{:T(128)}, f32[4,64,128]{2,1,0:T(8,128)S(1)}, f32[4]{0:T(128)S(1)}, f32[4,4,64,128]{3,2,1,0:T(8,128)}, f32[4,4]{1,0:T(4,128)S(1)}, /*index=5*/...) while((s32[]{:T(128)}, f32[4,64,128]{2,1,0:T(8,128)S(1)}, f32[4]{0:T(128)S(1)}, ...), condition=%wide.region_7.8_spmd.clone, body=%wide.region_6.7_spmd.clone.sunk | while | flops 131083 | bytes 656117 | solution.py:152
  335.6 12.6 %all-gather.1 = f32[16,64,128]{2,1,0:T(8,128)} all-gather(f32[4,64,128]{2,1,0:T(8,128)S(1)} %get-tuple-element.142), channel_id=3, replica_groups=mesh['seq'=4,'tp'=8] {'seq'}, dimensions={0}, use_global_device_ids=true | all-gather | bytes 655360 | tf_op jit(solution)/shard_map/all_gather | solution.py:29
  348.2 8.9 %all-reduce.1 = f32[16]{0:T(128)S(1)} all-reduce(f32[16]{0:T(128)S(1)} %dynamic-update-slice), channel_id=2, replica_groups=mesh['seq'=4,'tp'=8] {'seq'}, use_global_device_ids=true, to_apply=%add.1 | all-reduce | flops 16 | bytes 128
  357.2 3.1 while.32
  362.3 6.6 %fusion.41 = f32[4,256,4,64]{1,3,2,0:T(8,128)S(1)} fusion(f32[4,4,256]{2,1,0:T(4,128)S(1)} %copy.69, f32[4,256,256]{2,1,0:T(8,128)S(1)} %fusion.56, f32[4,4,256]{2,1,0:T(4,128)S(1)} %reduce_window_sum.41, pred[4,256,256]{2,1,0:T(8,128)(4,1)} %compare_and_fusion, f32[4,256,4,64]{1,0,3,2:T(4,128)} %reshape.145), kind=kOutput, calls=%fused_computation.61 | convolution fusion | flops 810549248 | bytes 3440640 | tf_op jit(solution)/shard_map/chij,cjhp->cihp/dot_general | solution.py:135
  372.8 8.2 %fusion.55 = f32[1024,4096]{1,0:T(8,128)} fusion(bf16[256,4096]{1,0:T(8,128)(2,1)S(1)} %copy-done, f32[1024,256]{0,1:T(8,128)S(1)} %get-tuple-element.213, f32[256]{0:T(256)S(1)} %copy-done.14, f32[1024]{0:T(1024)S(1)} %add_rsqrt_fusion), kind=kOutput, calls=%fused_computation.75 | convolution fusion | flops 2148270080 | bytes 19928064 | tf_op jit(solution)/shard_map/dot_general | solution.py:169
  381.1 165.9 %reduce-scatter.2.cloned.1.call-done = f32[128,4096]{1,0:T(8,128)} async-done(((f32[1024,4096]{1,0:T(8,128)}), f32[128,4096]{1,0:T(8,128)}) %reduce-scatter.2.cloned.1.call-update) | async-done | bytes 2097168 | tf_op jit(solution)/shard_map/reduce_scatter | solution.py:170
  547.0 2.8 fusion.31
  (147 shorter events, 44.8 us)
Async XLA Ops:
  6.5 366.3 %copy-start = (bf16[256,4096]{1,0:T(8,128)(2,1)S(1)}, bf16[256,4096]{1,0:T(8,128)(2,1)}, u32[]{:S(2)}) copy-start(bf16[256,4096]{1,0:T(8,128)(2,1)} %param.28) | copy-start | bytes 6291460
  6.5 540.4 %reduce-scatter.2.cloned.1.call-start = ((), (), s32[]{:S(2)}) async-start(), calls=%async_computation.1 | async-start | bytes 18874368 | tf_op jit(solution)/shard_map/reduce_scatter | solution.py:170
  10.8 16.8 %collective-permute-start.1 = (bf16[128,4096]{1,0:T(8,128)(2,1)S(1)}, bf16[128,4096]{1,0:T(8,128)(2,1)S(1)}, u32[]{:S(2)}, u32[]{:S(2)}) collective-permute-start(bf16[128,4096]{1,0:T(8,128)(2,1)S(1)} %get-tuple-element.218), channel_id=1, source_target_pairs={{0,7},{1,0},{2,1},{3,2},{4,3},{5,4},{6,5},{7,6},{8,15},{9,8},{10,9... | collective-permute-start | bytes 3145736 | tf_op jit(solution)/shard_map/ppermute | solution.py:94
  27.6 50.1 %copy-start.3 = (bf16[128,4096]{1,0:T(8,128)(2,1)}, bf16[128,4096]{1,0:T(8,128)(2,1)S(1)}, u32[]{:S(2)}) copy-start(bf16[128,4096]{1,0:T(8,128)(2,1)S(1)} %collective-permute-done.1) | copy-start | bytes 3145732
  27.8 51.2 %copy-start.18 = (bf16[4,128]{1,0:T(4,128)(2,1)S(1)}, bf16[4,128]{1,0:T(4,128)(2,1)}, u32[]{:S(2)}) copy-start(bf16[4,128]{1,0:T(4,128)(2,1)} %param.25) | copy-start | bytes 3076
  27.8 51.2 %copy-start.12 = (s32[4096]{0:T(1024)S(1)}, s32[4096]{0:T(1024)}, u32[]{:S(2)}) copy-start(s32[4096]{0:T(1024)} %param.29) | copy-start | bytes 49156
  27.9 46.4 %collective-permute-start.2 = (bf16[256,4096]{1,0:T(8,128)(2,1)S(1)}, bf16[256,4096]{1,0:T(8,128)(2,1)S(1)}, u32[]{:S(2)}, u32[]{:S(2)}) collective-permute-start(bf16[256,4096]{1,0:T(8,128)(2,1)S(1)} %pad_maximum_fusion.4), channel_id=1, source_target_pairs={{0,6},{1,7},{2,0},{3,1},{4,2},{5,3},{6,4},{7,5},{8,14},{9,15},{10,... | collective-permute-start | bytes 6291464 | tf_op jit(solution)/shard_map/ppermute | solution.py:94
  77.8 183.8 %collective-permute-start.3 = (bf16[512,4096]{1,0:T(8,128)(2,1)}, bf16[512,4096]{1,0:T(8,128)(2,1)}, u32[]{:S(2)}, u32[]{:S(2)}) collective-permute-start(bf16[512,4096]{1,0:T(8,128)(2,1)} %pad_maximum_fusion), channel_id=1, source_target_pairs={{0,4},{1,5},{2,6},{3,7},{4,0},{5,1},{6,2},{7,3},{8,12},{9,13},{10,... | collective-permute-start | bytes 12582920 | tf_op jit(solution)/shard_map/ppermute | solution.py:94
  77.8 216.4 %collective-permute-start.4 = (bf16[4096,128]{1,0:T(8,128)(2,1)}, bf16[4096,128]{1,0:T(8,128)(2,1)}, u32[]{:S(2)}, u32[]{:S(2)}) collective-permute-start(bf16[4096,128]{1,0:T(8,128)(2,1)} %param.20), channel_id=1, source_target_pairs={{0,1},{1,0},{2,3},{3,2},{4,5},{5,4},{6,7},{7,6},{8,9},{9,8},{10,11... | collective-permute-start | bytes 3145736 | tf_op jit(solution)/shard_map/ppermute | solution.py:18
  79.0 9.5 %collective-permute-start = (bf16[4,128]{1,0:T(4,128)(2,1)S(1)}, bf16[4,128]{1,0:T(4,128)(2,1)S(1)}, u32[]{:S(2)}, u32[]{:S(2)}) collective-permute-start(bf16[4,128]{1,0:T(4,128)(2,1)S(1)} %copy-done.18), channel_id=1, source_target_pairs={{0,1},{1,0},{2,3},{3,2},{4,5},{5,4},{6,7},{7,6},{8,9},{9,8},{10,11... | collective-permute-start | bytes 3080 | tf_op jit(solution)/shard_map/ppermute | solution.py:18
  82.2 4.9 copy-start.19
  82.2 5.1 copy-start.20
  82.2 6.3 %copy-start.17 = (bf16[4,256]{1,0:T(4,128)(2,1)S(1)}, bf16[4,256]{1,0:T(4,128)(2,1)}, u32[]{:S(2)}) copy-start(bf16[4,256]{1,0:T(4,128)(2,1)} %param.24) | copy-start | bytes 6148
  94.0 173.4 %copy-start.4 = (bf16[128,4096]{1,0:T(8,128)(2,1)S(1)}, bf16[128,4096]{1,0:T(8,128)(2,1)}, u32[]{:S(2)}) copy-start(bf16[128,4096]{1,0:T(8,128)(2,1)} %copy-done.3) | copy-start | bytes 3145732
  269.9 4.7 copy-start.13
  269.9 4.7 copy-start.15
  269.9 4.7 copy-start.16
  294.2 17.7 %copy-start.7 = (f32[1024,512]{0,1:T(8,128)}, f32[1024,512]{0,1:T(8,128)S(1)}, u32[]{:S(2)}) copy-start(f32[1024,512]{0,1:T(8,128)S(1)} %fusion.10) | copy-start | bytes 6291460
  308.2 9.2 %collective-permute-start.5 = (f32[3,512]{0,1:T(8,128)S(1)}, f32[3,512]{0,1:T(8,128)S(1)}, u32[]{:S(2)}, u32[]{:S(2)}) collective-permute-start(f32[3,512]{0,1:T(8,128)S(1)} %pad_maximum_fusion.5), channel_id=1, source_target_pairs={{0,8},{8,16},{16,24},{1,9},{9,17},{17,25},{2,10},{10,18},{18,26},{... | collective-permute-start | bytes 18440 | tf_op jit(solution)/shard_map/ppermute | solution.py:24
  362.3 6.6 %copy-start.10 = (f32[4,256,128]{1,0,2:T(4,128)S(1)}, f32[4,256,128]{1,0,2:T(4,128)}, u32[]{:S(2)}) copy-start(f32[4,256,128]{1,0,2:T(4,128)} %reshape.149) | copy-start | bytes 1572868
  362.3 6.6 %copy-start.11 = (f32[4,4,64,128]{3,2,1,0:T(8,128)S(1)}, f32[4,4,64,128]{3,2,1,0:T(8,128)}, u32[]{:S(2)}) copy-start(f32[4,4,64,128]{3,2,1,0:T(8,128)} %get-tuple-element.139) | copy-start | bytes 1572868
  370.1 2.7 copy-start.14
  371.6 1.2 collective-permute-start.6
  381.1 165.9 %copy-start.9 = (bf16[128,4096]{1,0:T(8,128)(2,1)S(1)}, bf16[128,4096]{1,0:T(8,128)(2,1)}, u32[]{:S(2)}) copy-start(bf16[128,4096]{1,0:T(8,128)(2,1)} %param.17) | copy-start | bytes 3145732
  (5 other events, 9.5 us)
Sparse Core Ops, SparseCore 0:
  381.2 165.7 reduce-scatter.1
